TPU v7x, 32 devices: a whole 2x2x4 slice. The times are simulated.
32 devices in a mesh: seq: 8 (over z, x), head: 4 (over y, core).
Axes of the slice: x: 2, y: 2, z: 4, core: 2. Of those that a mesh axis runs over, the one named last changes fastest.
Arguments:
- x_points: bfloat16 [16384, 512], P('seq', 'head'), may hold values from -6 to 6
- hilbert_index: int32 [16384], P('seq'), may hold values from 0 to 16383, as said below
- w_qkv: bfloat16 [2, 512, 3, 512], P(None, None, None, 'head'), may hold values from -3 to 3
- w_out: bfloat16 [2, 512, 512], P(None, 'head'), may hold values from -0.25 to 0.25
- w_up: bfloat16 [2, 2048, 512], P(None, 'head'), may hold values from -0.25 to 0.25
- w_down: bfloat16 [2, 2048, 512], P(None, 'head'), may hold values from -0.125 to 0.125
Outputs:
- z_out: bfloat16 [16384, 512], P('seq', 'head')
Inputs may be any that keep to these rules, and one draw needn't show every extreme that they name: `hilbert_index`: A permutation of all point positions. Call rows k * 2048 to (k + 1) * 2048 - 1 of either order shard k; the first and the last shard count as next to each other. Of the points of Z-order shard k, at most 1376 have a Hilbert position in shard k, at most 384 in each of the shards k - 1 and k + 1, and exactly 32 in every other shard. Some shard keeps exactly 1376, and some pair of neighbouring shards reaches 384 in both directions.
All inputs are finite; a program needn't handle non-finite values.
Results may differ from a plain program's by a relative error of at most 0.025.
Values may be sent and summed in bfloat16 or wider, within the bound.
A program may use at most 64 MiB of HBM per device.

v0:
```python
import functools
import math

import jax
import jax.numpy as jnp
from jax import lax
from jax.experimental import pallas as pl
from jax.experimental.pallas import tpu as pltpu
from jax.sharding import PartitionSpec as P

HEAD_DIM = 32
PATCH = 1024
EPS = 1e-05
LANES = 128
BASE = 64
MESH = pl.DeviceIdType.MESH
F32 = jnp.float32
BF16 = jnp.bfloat16


def block(index, size):
    return pl.ds(pl.multiple_of(index * size, size), size)


def norm(values):
    center = values - jnp.mean(values, axis=-1, keepdims=True)
    spread = jnp.mean(center * center, axis=-1, keepdims=True)
    return (center * lax.rsqrt(spread + EPS)).astype(BF16)


def matmul(a, b):
    return jnp.dot(a, b, preferred_element_type=F32)


def matmul_nt(a, b):
    return lax.dot_general(a, b, (((1,), (1,)), ((), ())), preferred_element_type=F32)


def gelu(x):
    return 0.5 * x * (1.0 + lax.erf(x * math.sqrt(0.5)))


def chosen_rows(count, base, index_row):
    slots = lax.broadcasted_iota(jnp.int32, (count, index_row.shape[1]), 0) + base
    return (slots == index_row).astype(F32).astype(BF16)


def chosen_cols(index_col, count):
    slots = lax.broadcasted_iota(jnp.int32, (index_col.shape[0], count), 1)
    return (slots == index_col).astype(F32).astype(BF16)


QKV, OUT, UP, DOWN = 2, 3, 4, 5


def program_kernel(
    n_head, peers, near, cap,
    x_ref, wqkv_ref, wout_ref, wup_ref, wdown_ref, index_ref,
    final_ref,
    rows, wqkv, wout, wup, wdown, normed, q, k, v, attended, mid_norm, result, cols, moved,
    pick, keep, spread, near_out, far_out, near_in, far_in, got, codes, partial, code_ref,
    local_sem, send_sem, recv_sem, out_send, out_recv, seq_send, seq_recv,
):
    me = lax.axis_index("head")
    seq = lax.axis_index("seq")
    side = lax.rem(seq, 2)
    neighbour = seq + 1 - 2 * side
    sibling = me + 1 - 2 * lax.rem(me, 2)
    partner = lax.rem(me + n_head // 2, n_head)
    half = lax.rem(me, 2)
    own_rows, width = result.shape
    points = moved.shape[0]
    slots = 2 * near + peers * cap
    chunk = PATCH // 2

    barrier = pltpu.get_barrier_semaphore()
    for step in range(1, n_head):
        to = lax.rem(me + step, n_head)
        pl.semaphore_signal(barrier, inc=1, device_id={"head": to}, device_id_type=MESH)
    for step in range(1, peers):
        to = lax.rem(seq + step, peers)
        pl.semaphore_signal(barrier, inc=1, device_id={"seq": to}, device_id_type=MESH)
    pl.semaphore_wait(barrier, n_head + peers - 2)

    def source(l, i, to):
        if i < 2:
            start = pl.multiple_of((to // 2) * PATCH + i * chunk, chunk)
            return (x_ref if l == 0 else moved).at[pl.ds(start, chunk)]
        return (wqkv_ref, wout_ref, wup_ref, wdown_ref)[i - QKV].at[l]

    def place(l, i, owner):
        if i < 2:
            return rows.at[l, pl.ds(i * chunk, chunk), block(owner, LANES)]
        if i == QKV:
            return wqkv.at[l, :, :, block(owner, LANES)]
        ref = (wout, wup, wdown)[i - OUT]
        return ref.at[l, block(owner, ref.shape[1] // n_head)]

    def part(i, ref, which):
        if i < 2:
            return ref
        if i == QKV:
            return ref.at[:, block(which, ref.shape[1] // 2)]
        return ref.at[block(which, ref.shape[0] // 2)]

    def own(l, i):
        return pltpu.make_async_copy(source(l, i, me), place(l, i, me), local_sem.at[l, i])

    def remote(l, i, way, src, dst, device):
        return pltpu.make_async_remote_copy(
            src_ref=src,
            dst_ref=dst,
            send_sem=send_sem.at[l, i, way],
            recv_sem=recv_sem.at[l, i, way],
            device_id=device,
            device_id_type=MESH,
        )

    def to_partner(l, i):
        src = part(i, source(l, i, partner), side)
        return remote(l, i, 0, src, part(i, place(l, i, me), side), {"head": partner})

    def to_sibling(l, i):
        return remote(l, i, 1, source(l, i, sibling), place(l, i, me), {"head": sibling})

    def forward(l, i):
        ref = part(i, place(l, i, partner), side)
        return remote(l, i, 2, ref, ref, {"head": sibling})

    def to_neighbour(l, i):
        ref = part(i, place(l, i, partner), side)
        return remote(l, i, 3, ref, ref, {"seq": neighbour})

    def forward_other(l, i):
        ref = part(i, place(l, i, partner), 1 - side)
        return remote(l, i, 4, ref, ref, {"head": sibling})

    def send(l, i):
        to_partner(l, i).start()
        own(l, i).start()

    def relay(l, i):
        to_partner(l, i).wait_recv()
        if i >= QKV:
            to_neighbour(l, i).start()
        forward(l, i).start()

    def relay_other(l, i):
        to_neighbour(l, i).wait_recv()
        forward_other(l, i).start()

    def ready(l, i):
        own(l, i).wait()
        to_sibling(l, i).wait_recv()
        forward(l, i).wait_recv()
        if i >= QKV:
            forward_other(l, i).wait_recv()

    def seq_copy(turn, step):
        to = lax.rem(seq + step, peers)
        back = turn == 2
        if step == 1:
            at = pl.ds(near if back else 0, near)
            src, dst = near_out.at[turn, at], near_in.at[turn, at]
        elif step == peers - 1:
            at = pl.ds(0 if back else near, near)
            src, dst = near_out.at[turn, at], near_in.at[turn, at]
        else:
            src, dst = far_out.at[turn, to], far_in.at[turn, seq]
        return pltpu.make_async_remote_copy(
            src_ref=src,
            dst_ref=dst,
            send_sem=seq_send.at[turn, step],
            recv_sem=seq_recv.at[turn, step],
            device_id={"seq": to},
            device_id_type=MESH,
        )

    def seq_send_rows(turn, table):
        for lo in range(0, 2 * near, near):
            near_out[turn, lo : lo + near] = matmul(pick[lo : lo + near], table).astype(BF16)
            seq_copy(turn, (1 if lo == 0 else peers - 1) if turn != 2 else (peers - 1 if lo == 0 else 1)).start()
        packed = matmul(pick[2 * near :], table)
        for peer in range(peers):
            far_out[turn, peer] = packed[peer * cap : (peer + 1) * cap].astype(BF16)
        for step in range(2, peers - 1):
            seq_copy(turn, step).start()

    def seq_receive(turn):
        for step in range(1, peers):
            seq_copy(turn, step).wait_recv()
        for step in (0, 1, peers - 1):
            unused = lax.rem(seq + step, peers)
            far_in[turn, unused] = jnp.zeros(far_in.shape[2:], BF16)
        got[: 2 * near] = near_in[turn]
        for peer in range(peers):
            at = 2 * near + peer * cap
            got[at : at + cap] = far_in[turn, peer].astype(F32).astype(BF16)

    def normalise(l, i):
        @pl.loop(0, chunk // LANES)
        def _(j):
            at = pl.ds(pl.multiple_of(i * chunk + j * LANES, LANES), LANES)
            normed[at] = norm(rows[l, at].astype(F32))

    def keys_values(l, i):
        @pl.loop(0, chunk // 256)
        def _(j):
            at = pl.ds(pl.multiple_of(i * chunk + j * 256, 256), 256)
            k[at] = matmul(normed[at], wqkv[l, 1]).astype(BF16)
            v[at] = matmul(normed[at], wqkv[l, 2]).astype(BF16)

    def queries(l):
        scale = HEAD_DIM ** (-0.5) * math.log2(math.e)

        @pl.loop(0, own_rows // 256)
        def _(j):
            mine = pl.ds(pl.multiple_of(half * own_rows + j * 256, 256), 256)
            q[block(j, 256)] = (matmul(normed[mine], wqkv[l, 0]) * scale).astype(BF16)

    def attend(group):
        group_cols = pl.ds(group * LANES, LANES)
        owner = lax.broadcasted_iota(jnp.int32, (PATCH, LANES), 1) // HEAD_DIM

        @pl.loop(0, own_rows // 256)
        def _(i):
            at = block(i, 256)
            query = q[at, group_cols]
            key = k[:, group_cols]
            value = v[:, group_cols]
            sums = jnp.zeros((256, LANES), F32)
            for head in range(LANES // HEAD_DIM):
                chosen = owner == head
                scores = matmul_nt(query, jnp.where(chosen, key, jnp.zeros_like(key)))
                top = jnp.max(scores, axis=-1, keepdims=True)
                weights = jnp.exp2(scores - top).astype(BF16)
                wide = jnp.concatenate(
                    [jnp.where(chosen, value, jnp.zeros_like(value)), jnp.ones_like(value)], axis=1
                )
                mixed = matmul(weights, wide)
                sums = sums + mixed[:, :LANES] / mixed[:, LANES:]
            attended[at, group_cols] = sums.astype(BF16)

    def out_copy(l, piece, step):
        to = lax.rem(me + step, n_head)
        at = pl.ds(pl.multiple_of(me * own_rows + piece * 256, 256), 256)
        return pltpu.make_async_remote_copy(
            src_ref=result.at[block(piece, 256), block(to, LANES)],
            dst_ref=cols.at[l, at],
            send_sem=out_send.at[l, piece, step],
            recv_sem=out_recv.at[l, piece, step],
            device_id={"head": to},
            device_id_type=MESH,
        )

    hidden = wup.shape[1]
    hidden_cols = 512

    def feed_forward(l):
        for piece in range(own_rows // 256):
            at = pl.ds(piece * 256, 256)
            mine = pl.ds(pl.multiple_of(half * own_rows + piece * 256, 256), 256)
            summed = (rows[l, mine].astype(F32) + matmul(attended[at], wout[l])).astype(BF16)
            total = summed.astype(F32)
            mid_norm[at] = norm(total)
            partial[...] = total

            @pl.loop(0, hidden // hidden_cols)
            def _(j):
                hid = block(j, hidden_cols)
                inner = gelu(matmul_nt(mid_norm[at], wup[l, hid])).astype(BF16)
                partial[...] += matmul(inner, wdown[l, hid])

            result[at] = partial[...].astype(BF16)
            for step in range(2, n_head):
                out_copy(l, piece, step).start()
            out_copy(l, piece, 1).start()
            cols[l, pl.ds(pl.multiple_of(me * own_rows + piece * 256, 256), 256)] = result[
                at, block(me, LANES)
            ]

    def out_wait(l):
        for piece in range(own_rows // 256):
            for step in range(1, n_head):
                out_copy(l, piece, step).wait()

    for i in range(6):
        send(0, i)
        if i < 2:
            to_sibling(0, i).start()
    send(1, QKV)
    send(1, OUT)

    where_to = index_ref[...]
    bounds = lax.broadcasted_iota(jnp.int32, (peers, points), 0) * points
    hot = jnp.where((where_to >= bounds) & (where_to < bounds + points), 1.0, 0.0)
    lower = lax.broadcasted_iota(jnp.int32, (LANES, LANES), 0)
    upper = lax.broadcasted_iota(jnp.int32, (LANES, LANES), 1)
    triangle = jnp.where(lower <= upper, 1.0, 0.0).astype(BF16)
    carried = jnp.zeros((peers, 1), F32)
    counts = []
    for at in range(0, points, LANES):
        piece = hot[:, at : at + LANES]
        counts.append(matmul(piece.astype(BF16), triangle) + carried)
        carried = carried + jnp.sum(piece, axis=1, keepdims=True)
    rank = jnp.sum(jnp.concatenate(counts, axis=1) * hot, axis=0, keepdims=True)
    rank = rank.astype(jnp.int32) - 1
    device_start = jnp.sum(hot * bounds.astype(F32), axis=0, keepdims=True).astype(jnp.int32)
    order = lax.broadcasted_iota(jnp.int32, (peers, points), 0).astype(F32)
    device = jnp.sum(hot * order, axis=0, keepdims=True).astype(jnp.int32)
    row = where_to - device_start
    following = lax.rem(seq + 1, peers)
    previous = lax.rem(seq + peers - 1, peers)
    slot = jnp.where(device == previous, near + rank, 2 * near + device * cap + rank)
    slot = jnp.where(device == following, rank, slot)
    slot = jnp.where(device == seq, -1, slot)
    kept = jnp.where(device == seq, row, -1)
    coded = row + BASE
    high = lax.shift_right_logical(coded, jnp.full_like(coded, BASE.bit_length() - 1))
    low = coded - high * BASE
    lane = lax.broadcasted_iota(jnp.int32, (LANES, points), 0)
    fields = jnp.where(lane == 2, slot, jnp.where(lane == 3, kept, 0))
    fields = jnp.where(lane == 0, high, jnp.where(lane == 1, low, fields))
    code_ref[...] = jnp.transpose(fields.astype(F32), (1, 0))

    @pl.loop(0, slots // LANES)
    def _(i):
        pick[block(i, LANES)] = chosen_rows(LANES, i * LANES, slot)

    relay(0, 0)
    seq_send_rows(0, code_ref[...].astype(BF16))
    relay(0, 1)
    to_sibling(0, QKV).start()
    ready(0, 0)
    normalise(0, 0)
    ready(0, 1)
    normalise(0, 1)
    seq_receive(0)
    codes[...] = got[...].astype(F32)
    turned = jnp.transpose(codes[...], (1, 0))
    target = (turned[0:1] * BASE + turned[1:2]).astype(jnp.int32) - BASE

    @pl.loop(0, points // LANES)
    def _(i):
        spread[block(i, LANES)] = chosen_rows(LANES, i * LANES, target)

    relay(0, QKV)

    @pl.loop(0, points // LANES)
    def _(i):
        keep[block(i, LANES)] = chosen_rows(LANES, i * LANES, kept)

    relay_other(0, QKV)
    to_sibling(0, OUT).start()
    ready(0, QKV)
    queries(0)
    keys_values(0, 0)
    keys_values(0, 1)
    relay(0, OUT)
    to_sibling(0, UP).start()
    attend(0)
    relay_other(0, OUT)
    to_sibling(0, DOWN).start()
    attend(1)
    relay(0, UP)
    attend(2)
    relay_other(0, UP)
    relay(0, DOWN)
    for group in range(3, width // LANES):
        attend(group)
    relay_other(0, DOWN)
    to_sibling(1, QKV).start()
    to_sibling(1, OUT).start()
    relay(1, QKV)
    ready(0, OUT)
    ready(0, UP)
    ready(0, DOWN)
    feed_forward(0)
    send(1, UP)
    to_sibling(1, UP).start()
    relay_other(1, QKV)
    relay(1, OUT)
    out_wait(0)

    seq_send_rows(1, cols[0])
    relay_other(1, OUT)
    moved[...] = matmul(keep[...], cols[0]).astype(BF16)
    seq_receive(1)
    moved[...] = (moved[...].astype(F32) + matmul(spread[...], got[...])).astype(BF16)

    for i in (0, 1, DOWN):
        send(1, i)
        to_sibling(1, i).start()

    @pl.loop(0, slots // LANES)
    def _(i):
        at = block(i, LANES)
        both = codes[at]
        place_col = (both[:, 0:1] * BASE + both[:, 1:2]).astype(jnp.int32) - BASE
        pick[at] = chosen_cols(place_col, points)

    relay(1, UP)
    relay(1, 0)
    relay(1, 1)
    ready(1, 0)
    normalise(1, 0)
    ready(1, QKV)
    keys_values(1, 0)
    ready(1, 1)
    normalise(1, 1)
    keys_values(1, 1)
    queries(1)
    relay_other(1, UP)
    attend(0)
    attend(1)
    relay(1, DOWN)
    attend(2)
    relay_other(1, DOWN)
    for group in range(3, width // LANES):
        attend(group)
    ready(1, OUT)
    ready(1, UP)
    ready(1, DOWN)
    feed_forward(1)

    @pl.loop(0, points // LANES)
    def _(i):
        at = block(i, LANES)
        keep[at] = chosen_cols(code_ref[at, 3:4].astype(jnp.int32), points)

    out_wait(1)
    seq_send_rows(2, cols[1])

    @pl.loop(0, points // LANES)
    def _(i):
        at = block(i, LANES)
        spread[at] = chosen_cols(code_ref[at, 2:3].astype(jnp.int32), slots)

    for i in range(QKV):
        to_partner(1, i).wait_send()
        to_sibling(1, i).wait_send()
    moved[...] = matmul(keep[...], cols[1]).astype(BF16)
    seq_receive(2)
    final_ref[...] = (moved[...].astype(F32) + matmul(spread[...], got[...])).astype(BF16)

    for l in range(2):
        for i in range(6):
            if l == 0 or i >= QKV:
                to_partner(l, i).wait_send()
                to_sibling(l, i).wait_send()
            forward(l, i).wait_send()
            if i >= QKV:
                to_neighbour(l, i).wait_send()
                forward_other(l, i).wait_send()
    for turn in range(3):
        for step in range(1, peers):
            seq_copy(turn, step).wait_send()


def on_device(peers, n_head, x_points, hilbert_index, w_qkv, w_out, w_up, w_down):
    points, cols = x_points.shape
    near = 3 * points // 16
    cap = points // (8 * peers)
    slots = 2 * near + peers * cap
    vmem = pl.BlockSpec(memory_space=pltpu.VMEM)
    w_qkv = jnp.transpose(w_qkv, (0, 2, 1, 3))

    width = cols * n_head
    own_rows = points // n_head
    hidden = w_up.shape[1] * n_head
    layers = w_up.shape[0]
    hbm = pl.BlockSpec(memory_space=pl.ANY)
    return pl.pallas_call(
        functools.partial(program_kernel, n_head, peers, near, cap),
        out_shape=jax.ShapeDtypeStruct((points, cols), BF16),
        in_specs=[hbm] * 5 + [vmem],
        out_specs=vmem,
        scratch_shapes=[
            pltpu.VMEM((layers, PATCH, width), BF16),
            pltpu.VMEM((layers, 3, width, width), BF16),
            pltpu.VMEM((layers, width, width), BF16),
            pltpu.VMEM((layers, hidden, width), BF16),
            pltpu.VMEM((layers, hidden, width), BF16),
            pltpu.VMEM((PATCH, width), BF16),
            pltpu.VMEM((own_rows, width), BF16),
            pltpu.VMEM((PATCH, width), BF16),
            pltpu.VMEM((PATCH, width), BF16),
            pltpu.VMEM((own_rows, width), BF16),
            pltpu.VMEM((own_rows, width), BF16),
            pltpu.VMEM((own_rows, width), BF16),
            pltpu.VMEM((layers, points, cols), BF16),
            pltpu.VMEM((points, cols), BF16),
            pltpu.VMEM((slots, points), BF16),
            pltpu.VMEM((points, points), BF16),
            pltpu.VMEM((points, slots), BF16),
            pltpu.VMEM((3, 2 * near, cols), BF16),
            pltpu.VMEM((3, peers, cap, cols), BF16),
            pltpu.VMEM((3, 2 * near, cols), BF16),
            pltpu.VMEM((3, peers, cap, cols), BF16),
            pltpu.VMEM((slots, cols), BF16),
            pltpu.VMEM((slots, cols), F32),
            pltpu.VMEM((256, width), F32),
            pltpu.VMEM((points, LANES), F32),
            pltpu.SemaphoreType.DMA((layers, 6)),
            pltpu.SemaphoreType.DMA((layers, 6, 5)),
            pltpu.SemaphoreType.DMA((layers, 6, 5)),
            pltpu.SemaphoreType.DMA((layers, own_rows // 256, n_head)),
            pltpu.SemaphoreType.DMA((layers, own_rows // 256, n_head)),
            pltpu.SemaphoreType.DMA((3, peers)),
            pltpu.SemaphoreType.DMA((3, peers)),
        ],
        compiler_params=pltpu.CompilerParams(
            collective_id=0, has_side_effects=True, vmem_limit_bytes=60 * 1024 * 1024
        ),
        name="point_layers",
    )(x_points, w_qkv, w_out, w_up, w_down, hilbert_index.reshape(1, points))


def solution(mesh):
    return jax.shard_map(
        functools.partial(on_device, mesh.shape["seq"], mesh.shape["head"]),
        mesh=mesh,
        in_specs=(
            P("seq", "head"),
            P("seq"),
            P(None, None, None, "head"),
            P(None, "head", None),
            P(None, "head", None),
            P(None, "head", None),
        ),
        out_specs=P("seq", "head"),
        check_vma=False,
    )
```

profile of v0, /device:TPU:0, one launch (start us, length us, event | category | flops | bytes accessed | tf_op | source)
XLA Modules:
  0.0 125.0 jit_solution(16393632778333169871)
XLA Ops:
  0.0 123.1 %point_layers.1 = bf16[2048,128]{1,0:T(8,128)(2,1)} custom-call(bf16[2048,128]{1,0:T(8,128)(2,1)} %x_ref.1, bf16[2,3,512,128]{3,2,1,0:T(8,128)(2,1)} %bitcast.2, bf16[2,128,512]{2,1,0:T(8,128)(2,1)} %wout_ref.1, bf16[2,512,512]{2,1,0:T(8,128)(2,1)} %wup_ref.1, bf16[2,512,512]{2,1,0:T(8,128)(2,1)} %wdown_ref.1, s32[1,2048]{1,0:T(1,128)} %bitcast.3), custom_call_target="tpu_custom_call" | custom-call | tf_op jit(solution)/shard_map/point_layers/pallas_call | solution.py:473
  123.1 1.9 %copy.8 = bf16[2048,128]{1,0:T(8,128)(2,1)} copy(bf16[2048,128]{1,0:T(8,128)(2,1)} %point_layers.1) | data formatting | bytes 1048576
where the time goes:
time: 125 us
  Pallas kernels  123 us (98%)
  local copies, waits for them, and re-layouts  1.87 us (1%)
    pallas_call x1, Pallas kernels, on_device(): pl.pallas_call(functools.partial(program_kernel, n_head, peers, near, cap...  123 us

commit v1 on v0

--- a/solution.py
+++ b/solution.py
@@ -92,7 +92,7 @@
         if i < 2:
             return rows.at[l, pl.ds(i * chunk, chunk), block(owner, LANES)]
         if i == QKV:
-            return wqkv.at[l, :, :, block(owner, LANES)]
+            return wqkv.at[l, owner // 2, :, :, block(lax.rem(owner, 2), LANES)]
         ref = (wout, wup, wdown)[i - OUT]
         return ref.at[l, block(owner, ref.shape[1] // n_head)]
 
@@ -203,43 +203,41 @@
             at = pl.ds(pl.multiple_of(i * chunk + j * LANES, LANES), LANES)
             normed[at] = norm(rows[l, at].astype(F32))
 
-    def keys_values(l, i):
-        @pl.loop(0, chunk // 256)
-        def _(j):
-            at = pl.ds(pl.multiple_of(i * chunk + j * 256, 256), 256)
-            k[at] = matmul(normed[at], wqkv[l, 1]).astype(BF16)
-            v[at] = matmul(normed[at], wqkv[l, 2]).astype(BF16)
-
-    def queries(l):
+    def keys_values(l, chip, i):
+        at = pl.ds(i * chunk, chunk)
+        keys = matmul(normed[at], wqkv[l, chip, 1]).astype(BF16)
+        values = matmul(normed[at], wqkv[l, chip, 2]).astype(BF16)
+        for part_of in range(2):
+            cut = slice(part_of * LANES, (part_of + 1) * LANES)
+            k[chip * 2 + part_of, at] = keys[:, cut]
+            v[chip * 2 + part_of, at, :LANES] = values[:, cut]
+
+    def queries(l, chip):
         scale = HEAD_DIM ** (-0.5) * math.log2(math.e)
-
-        @pl.loop(0, own_rows // 256)
-        def _(j):
-            mine = pl.ds(pl.multiple_of(half * own_rows + j * 256, 256), 256)
-            q[block(j, 256)] = (matmul(normed[mine], wqkv[l, 0]) * scale).astype(BF16)
-
-    def attend(group):
-        group_cols = pl.ds(group * LANES, LANES)
-        owner = lax.broadcasted_iota(jnp.int32, (PATCH, LANES), 1) // HEAD_DIM
-
-        @pl.loop(0, own_rows // 256)
-        def _(i):
-            at = block(i, 256)
-            query = q[at, group_cols]
-            key = k[:, group_cols]
-            value = v[:, group_cols]
-            sums = jnp.zeros((256, LANES), F32)
+        mine = pl.ds(pl.multiple_of(half * own_rows, own_rows), own_rows)
+        found = (matmul(normed[mine], wqkv[l, chip, 0]) * scale).astype(BF16)
+        for part_of in range(2):
+            q[chip * 2 + part_of] = found[:, part_of * LANES : (part_of + 1) * LANES]
+
+    def attend(chip, first, last):
+        owner = lax.broadcasted_iota(jnp.int32, (256, LANES), 1) // HEAD_DIM
+
+        @pl.loop(first, last)
+        def _(step):
+            group = chip * 2 + step // 2
+            at = block(lax.rem(step, 2), 256)
+            query = q[group, at]
+            total = jnp.zeros((256, LANES), F32)
+            norms = jnp.ones((256, LANES), F32)
             for head in range(LANES // HEAD_DIM):
                 chosen = owner == head
-                scores = matmul_nt(query, jnp.where(chosen, key, jnp.zeros_like(key)))
+                scores = matmul_nt(jnp.where(chosen, query, jnp.zeros_like(query)), k[group])
                 top = jnp.max(scores, axis=-1, keepdims=True)
                 weights = jnp.exp2(scores - top).astype(BF16)
-                wide = jnp.concatenate(
-                    [jnp.where(chosen, value, jnp.zeros_like(value)), jnp.ones_like(value)], axis=1
-                )
-                mixed = matmul(weights, wide)
-                sums = sums + mixed[:, :LANES] / mixed[:, LANES:]
-            attended[at, group_cols] = sums.astype(BF16)
+                mixed = matmul(weights, v[group])
+                total = jnp.where(chosen, mixed[:, :LANES], total)
+                norms = jnp.where(chosen, mixed[:, LANES:], norms)
+            attended[at, block(group, LANES)] = (total / norms).astype(BF16)
 
     def out_copy(l, piece, step):
         to = lax.rem(me + step, n_head)
@@ -286,7 +284,7 @@
 
     for i in range(6):
         send(0, i)
-        if i < 2:
+        if i < 3:
             to_sibling(0, i).start()
     send(1, QKV)
     send(1, OUT)
@@ -330,11 +328,21 @@
     relay(0, 0)
     seq_send_rows(0, code_ref[...].astype(BF16))
     relay(0, 1)
-    to_sibling(0, QKV).start()
+    for group in range(n_head):
+        v[group, :, LANES:] = jnp.ones((PATCH, LANES), BF16)
+    mine_chip = me // 2
+    other_chip = partner // 2
+    own(0, QKV).wait()
+    to_sibling(0, QKV).wait_recv()
     ready(0, 0)
     normalise(0, 0)
+    keys_values(0, mine_chip, 0)
     ready(0, 1)
     normalise(0, 1)
+    keys_values(0, mine_chip, 1)
+    queries(0, mine_chip)
+    relay(0, QKV)
+    to_sibling(0, OUT).start()
     seq_receive(0)
     codes[...] = got[...].astype(F32)
     turned = jnp.transpose(codes[...], (1, 0))
@@ -344,30 +352,29 @@
     def _(i):
         spread[block(i, LANES)] = chosen_rows(LANES, i * LANES, target)
 
-    relay(0, QKV)
+    attend(mine_chip, 0, 2)
+    relay(0, OUT)
+    to_sibling(0, UP).start()
+    attend(mine_chip, 2, 3)
+    relay_other(0, QKV)
+    to_sibling(0, DOWN).start()
+    attend(mine_chip, 3, 4)
+    relay_other(0, OUT)
 
     @pl.loop(0, points // LANES)
     def _(i):
         keep[block(i, LANES)] = chosen_rows(LANES, i * LANES, kept)
 
-    relay_other(0, QKV)
-    to_sibling(0, OUT).start()
-    ready(0, QKV)
-    queries(0)
-    keys_values(0, 0)
-    keys_values(0, 1)
-    relay(0, OUT)
-    to_sibling(0, UP).start()
-    attend(0)
-    relay_other(0, OUT)
-    to_sibling(0, DOWN).start()
-    attend(1)
+    forward(0, QKV).wait_recv()
+    forward_other(0, QKV).wait_recv()
+    for i in range(2):
+        keys_values(0, other_chip, i)
+    queries(0, other_chip)
     relay(0, UP)
-    attend(2)
+    attend(other_chip, 0, 2)
     relay_other(0, UP)
     relay(0, DOWN)
-    for group in range(3, width // LANES):
-        attend(group)
+    attend(other_chip, 2, 4)
     relay_other(0, DOWN)
     to_sibling(1, QKV).start()
     to_sibling(1, OUT).start()
@@ -405,19 +412,20 @@
     ready(1, 0)
     normalise(1, 0)
     ready(1, QKV)
-    keys_values(1, 0)
+    for chip in range(n_head // 2):
+        keys_values(1, chip, 0)
     ready(1, 1)
     normalise(1, 1)
-    keys_values(1, 1)
-    queries(1)
+    for chip in range(n_head // 2):
+        keys_values(1, chip, 1)
+    for chip in range(n_head // 2):
+        queries(1, chip)
     relay_other(1, UP)
-    attend(0)
-    attend(1)
+    attend(0, 0, 4)
     relay(1, DOWN)
-    attend(2)
+    attend(1, 0, 2)
     relay_other(1, DOWN)
-    for group in range(3, width // LANES):
-        attend(group)
+    attend(1, 2, 4)
     ready(1, OUT)
     ready(1, UP)
     ready(1, DOWN)
@@ -477,14 +485,14 @@
         out_specs=vmem,
         scratch_shapes=[
             pltpu.VMEM((layers, PATCH, width), BF16),
-            pltpu.VMEM((layers, 3, width, width), BF16),
+            pltpu.VMEM((layers, n_head // 2, 3, width, 2 * LANES), BF16),
             pltpu.VMEM((layers, width, width), BF16),
             pltpu.VMEM((layers, hidden, width), BF16),
             pltpu.VMEM((layers, hidden, width), BF16),
             pltpu.VMEM((PATCH, width), BF16),
-            pltpu.VMEM((own_rows, width), BF16),
-            pltpu.VMEM((PATCH, width), BF16),
-            pltpu.VMEM((PATCH, width), BF16),
+            pltpu.VMEM((n_head, own_rows, LANES), BF16),
+            pltpu.VMEM((n_head, PATCH, LANES), BF16),
+            pltpu.VMEM((n_head, PATCH, 2 * LANES), BF16),
             pltpu.VMEM((own_rows, width), BF16),
             pltpu.VMEM((own_rows, width), BF16),
             pltpu.VMEM((own_rows, width), BF16),

time: 125 us -> 118 us (0.944)
  Pallas kernels: 123 us -> 116 us
    pallas_call x1, Pallas kernels: 123 us -> 116 us  [on_device(): pl.pallas_call(functools.partial(program_kernel, n_head, peers, near, cap...]
where the time goes in v1:
time: 118 us
  Pallas kernels  116 us (98%)
  local copies, waits for them, and re-layouts  1.87 us (2%)
    pallas_call x1, Pallas kernels, on_device(): pl.pallas_call(functools.partial(program_kernel, n_head, peers, near, cap...  116 us

profile of v1, /device:TPU:0, one launch (start us, length us, event | category | flops | bytes accessed | tf_op | source)
XLA Modules:
  0.0 117.5 jit_solution(10608716785896401350)
XLA Ops:
  0.0 115.7 %point_layers.1 = bf16[2048,128]{1,0:T(8,128)(2,1)} custom-call(bf16[2048,128]{1,0:T(8,128)(2,1)} %x_ref.1, bf16[2,3,512,128]{3,2,1,0:T(8,128)(2,1)} %bitcast.2, bf16[2,128,512]{2,1,0:T(8,128)(2,1)} %wout_ref.1, bf16[2,512,512]{2,1,0:T(8,128)(2,1)} %wup_ref.1, bf16[2,512,512]{2,1,0:T(8,128)(2,1)} %wdown_ref.1, s32[1,2048]{1,0:T(1,128)} %bitcast.3), custom_call_target="tpu_custom_call" | custom-call | tf_op jit(solution)/shard_map/point_layers/pallas_call | solution.py:481
  115.7 1.9 %copy.8 = bf16[2048,128]{1,0:T(8,128)(2,1)} copy(bf16[2048,128]{1,0:T(8,128)(2,1)} %point_layers.1) | data formatting | bytes 1048576

commit v2 on v1

--- a/solution.py
+++ b/solution.py
@@ -219,25 +219,31 @@
         for part_of in range(2):
             q[chip * 2 + part_of] = found[:, part_of * LANES : (part_of + 1) * LANES]
 
-    def attend(chip, first, last):
-        owner = lax.broadcasted_iota(jnp.int32, (256, LANES), 1) // HEAD_DIM
-
-        @pl.loop(first, last)
+    def attend(first, count, between):
+        owner = lax.broadcasted_iota(jnp.int32, (own_rows, LANES), 1) // HEAD_DIM
+
+        @pl.loop(0, count)
         def _(step):
-            group = chip * 2 + step // 2
-            at = block(lax.rem(step, 2), 256)
-            query = q[group, at]
-            total = jnp.zeros((256, LANES), F32)
-            norms = jnp.ones((256, LANES), F32)
+            for turn, action in between.items():
+                pl.when(step == turn)(action)
+            group = first + step
+            query = q[group]
+
+            def scores_of(head):
+                return matmul_nt(jnp.where(owner == head, query, jnp.zeros_like(query)), k[group])
+
+            total = jnp.zeros((own_rows, LANES), F32)
+            norms = jnp.ones((own_rows, LANES), F32)
+            scores = scores_of(0)
             for head in range(LANES // HEAD_DIM):
-                chosen = owner == head
-                scores = matmul_nt(jnp.where(chosen, query, jnp.zeros_like(query)), k[group])
+                following = scores_of(head + 1) if head + 1 < LANES // HEAD_DIM else None
                 top = jnp.max(scores, axis=-1, keepdims=True)
                 weights = jnp.exp2(scores - top).astype(BF16)
                 mixed = matmul(weights, v[group])
-                total = jnp.where(chosen, mixed[:, :LANES], total)
-                norms = jnp.where(chosen, mixed[:, LANES:], norms)
-            attended[at, block(group, LANES)] = (total / norms).astype(BF16)
+                total = jnp.where(owner == head, mixed[:, :LANES], total)
+                norms = jnp.where(owner == head, mixed[:, LANES:], norms)
+                scores = following
+            attended[:, block(group, LANES)] = (total / norms).astype(BF16)
 
     def out_copy(l, piece, step):
         to = lax.rem(me + step, n_head)
@@ -352,32 +358,34 @@
     def _(i):
         spread[block(i, LANES)] = chosen_rows(LANES, i * LANES, target)
 
-    attend(mine_chip, 0, 2)
-    relay(0, OUT)
-    to_sibling(0, UP).start()
-    attend(mine_chip, 2, 3)
+    def relay_out():
+        relay(0, OUT)
+        to_sibling(0, UP).start()
+        to_sibling(0, DOWN).start()
+
+    attend(mine_chip * 2, 2, {1: relay_out})
     relay_other(0, QKV)
-    to_sibling(0, DOWN).start()
-    attend(mine_chip, 3, 4)
     relay_other(0, OUT)
 
     @pl.loop(0, points // LANES)
     def _(i):
         keep[block(i, LANES)] = chosen_rows(LANES, i * LANES, kept)
 
+    relay(0, UP)
     forward(0, QKV).wait_recv()
     forward_other(0, QKV).wait_recv()
     for i in range(2):
         keys_values(0, other_chip, i)
     queries(0, other_chip)
-    relay(0, UP)
-    attend(other_chip, 0, 2)
-    relay_other(0, UP)
-    relay(0, DOWN)
-    attend(other_chip, 2, 4)
-    relay_other(0, DOWN)
+
+    def relay_up_down():
+        relay_other(0, UP)
+        relay(0, DOWN)
+
+    attend(other_chip * 2, 2, {1: relay_up_down})
     to_sibling(1, QKV).start()
     to_sibling(1, OUT).start()
+    relay_other(0, DOWN)
     relay(1, QKV)
     ready(0, OUT)
     ready(0, UP)
@@ -420,12 +428,15 @@
         keys_values(1, chip, 1)
     for chip in range(n_head // 2):
         queries(1, chip)
-    relay_other(1, UP)
-    attend(0, 0, 4)
-    relay(1, DOWN)
-    attend(1, 0, 2)
-    relay_other(1, DOWN)
-    attend(1, 2, 4)
+    attend(
+        0,
+        n_head,
+        {
+            1: lambda: relay_other(1, UP),
+            2: lambda: relay(1, DOWN),
+            n_head - 1: lambda: relay_other(1, DOWN),
+        },
+    )
     ready(1, OUT)
     ready(1, UP)
     ready(1, DOWN)

time: 118 us -> 114 us (0.966)
  Pallas kernels: 116 us -> 112 us
    pallas_call x1, Pallas kernels: 116 us -> 112 us  [on_device(): pl.pallas_call(functools.partial(program_kernel, n_head, peers, near, cap...]
where the time goes in v2:
time: 114 us
  Pallas kernels  112 us (98%)
  local copies, waits for them, and re-layouts  1.87 us (2%)
    pallas_call x1, Pallas kernels, on_device(): pl.pallas_call(functools.partial(program_kernel, n_head, peers, near, cap...  112 us

profile of v2, /device:TPU:0, one launch (start us, length us, event | category | flops | bytes accessed | tf_op | source)
XLA Modules:
  0.0 113.9 jit_solution(12359228737763676202)
XLA Ops:
  0.0 112.0 %point_layers.1 = bf16[2048,128]{1,0:T(8,128)(2,1)} custom-call(bf16[2048,128]{1,0:T(8,128)(2,1)} %x_ref.1, bf16[2,3,512,128]{3,2,1,0:T(8,128)(2,1)} %bitcast.2, bf16[2,128,512]{2,1,0:T(8,128)(2,1)} %wout_ref.1, bf16[2,512,512]{2,1,0:T(8,128)(2,1)} %wup_ref.1, bf16[2,512,512]{2,1,0:T(8,128)(2,1)} %wdown_ref.1, s32[1,2048]{1,0:T(1,128)} %bitcast.3), custom_call_target="tpu_custom_call" | custom-call | tf_op jit(solution)/shard_map/point_layers/pallas_call | solution.py:492
  112.0 1.9 %copy.8 = bf16[2048,128]{1,0:T(8,128)(2,1)} copy(bf16[2048,128]{1,0:T(8,128)(2,1)} %point_layers.1) | data formatting | bytes 1048576

commit v3 on v2

--- a/solution.py
+++ b/solution.py
@@ -50,7 +50,10 @@
     return (slots == index_col).astype(F32).astype(BF16)
 
 
-QKV, OUT, UP, DOWN = 2, 3, 4, 5
+QKV, OUT = 2, 3
+UP = (4, 6)
+DOWN = (5, 7)
+ITEMS = 8
 
 
 def program_kernel(
@@ -59,12 +62,10 @@
     final_ref,
     rows, wqkv, wout, wup, wdown, normed, q, k, v, attended, mid_norm, result, cols, moved,
     pick, keep, spread, near_out, far_out, near_in, far_in, got, codes, partial, code_ref,
-    local_sem, send_sem, recv_sem, out_send, out_recv, seq_send, seq_recv,
+    met, local_sem, send_sem, recv_sem, out_send, out_recv, seq_send, seq_recv,
 ):
     me = lax.axis_index("head")
     seq = lax.axis_index("seq")
-    side = lax.rem(seq, 2)
-    neighbour = seq + 1 - 2 * side
     sibling = me + 1 - 2 * lax.rem(me, 2)
     partner = lax.rem(me + n_head // 2, n_head)
     half = lax.rem(me, 2)
@@ -77,24 +78,50 @@
     for step in range(1, n_head):
         to = lax.rem(me + step, n_head)
         pl.semaphore_signal(barrier, inc=1, device_id={"head": to}, device_id_type=MESH)
-    for step in range(1, peers):
-        to = lax.rem(seq + step, peers)
-        pl.semaphore_signal(barrier, inc=1, device_id={"seq": to}, device_id_type=MESH)
-    pl.semaphore_wait(barrier, n_head + peers - 2)
+    rounds = peers.bit_length() - 1
+
+    def across(turn):
+        return seq + 2**turn - 2 ** (turn + 1) * lax.rem(seq // 2**turn, 2)
+
+    def greet(sem, turn):
+        pl.semaphore_signal(sem, inc=1, device_id={"seq": across(turn)}, device_id_type=MESH)
+
+    for turn in range(rounds):
+        greet(barrier, turn)
+    pl.semaphore_wait(barrier, n_head - 1 + rounds)
+
+    def entered(turn):
+        pl.semaphore_wait(met.at[turn], 1)
+        if turn + 1 < rounds:
+            greet(met.at[turn + 1], turn + 1)
+
+    def side_of(i):
+        return lax.rem(seq // 2, 2) if i in (UP[1], DOWN[1]) else lax.rem(seq, 2)
+
+    def neighbour_of(i):
+        return across(1) if i in (UP[1], DOWN[1]) else across(0)
+
+    hidden = wup.shape[1]
+    hidden_half = hidden // n_head // 2
 
     def source(l, i, to):
         if i < 2:
             start = pl.multiple_of((to // 2) * PATCH + i * chunk, chunk)
             return (x_ref if l == 0 else moved).at[pl.ds(start, chunk)]
-        return (wqkv_ref, wout_ref, wup_ref, wdown_ref)[i - QKV].at[l]
+        if i in (QKV, OUT):
+            return (wqkv_ref if i == QKV else wout_ref).at[l]
+        ref, turn = (wup_ref, UP.index(i)) if i in UP else (wdown_ref, DOWN.index(i))
+        return ref.at[l, pl.ds(turn * hidden_half, hidden_half)]
 
     def place(l, i, owner):
         if i < 2:
             return rows.at[l, pl.ds(i * chunk, chunk), block(owner, LANES)]
         if i == QKV:
             return wqkv.at[l, owner // 2, :, :, block(lax.rem(owner, 2), LANES)]
-        ref = (wout, wup, wdown)[i - OUT]
-        return ref.at[l, block(owner, ref.shape[1] // n_head)]
+        if i == OUT:
+            return wout.at[l, block(owner, wout.shape[1] // n_head)]
+        ref, turn = (wup, UP.index(i)) if i in UP else (wdown, DOWN.index(i))
+        return ref.at[l, block((owner // 2 * 2 + turn) * 2 + lax.rem(owner, 2), hidden_half)]
 
     def part(i, ref, which):
         if i < 2:
@@ -117,22 +144,22 @@
         )
 
     def to_partner(l, i):
-        src = part(i, source(l, i, partner), side)
-        return remote(l, i, 0, src, part(i, place(l, i, me), side), {"head": partner})
+        src = part(i, source(l, i, partner), side_of(i))
+        return remote(l, i, 0, src, part(i, place(l, i, me), side_of(i)), {"head": partner})
 
     def to_sibling(l, i):
         return remote(l, i, 1, source(l, i, sibling), place(l, i, me), {"head": sibling})
 
     def forward(l, i):
-        ref = part(i, place(l, i, partner), side)
+        ref = part(i, place(l, i, partner), side_of(i))
         return remote(l, i, 2, ref, ref, {"head": sibling})
 
     def to_neighbour(l, i):
-        ref = part(i, place(l, i, partner), side)
-        return remote(l, i, 3, ref, ref, {"seq": neighbour})
+        ref = part(i, place(l, i, partner), side_of(i))
+        return remote(l, i, 3, ref, ref, {"seq": neighbour_of(i)})
 
     def forward_other(l, i):
-        ref = part(i, place(l, i, partner), 1 - side)
+        ref = part(i, place(l, i, partner), 1 - side_of(i))
         return remote(l, i, 4, ref, ref, {"head": sibling})
 
     def send(l, i):
@@ -149,12 +176,18 @@
         to_neighbour(l, i).wait_recv()
         forward_other(l, i).start()
 
-    def ready(l, i):
+    def near_ready(l, i):
         own(l, i).wait()
         to_sibling(l, i).wait_recv()
+
+    def far_ready(l, i):
         forward(l, i).wait_recv()
         if i >= QKV:
             forward_other(l, i).wait_recv()
+
+    def ready(l, i):
+        near_ready(l, i)
+        far_ready(l, i)
 
     def seq_copy(turn, step):
         to = lax.rem(seq + step, peers)
@@ -257,10 +290,9 @@
             device_id_type=MESH,
         )
 
-    hidden = wup.shape[1]
-    hidden_cols = 512
-
-    def feed_forward(l):
+    hidden_cols = hidden // n_head
+
+    def feed_forward(l, between):
         for piece in range(own_rows // 256):
             at = pl.ds(piece * 256, 256)
             mine = pl.ds(pl.multiple_of(half * own_rows + piece * 256, 256), 256)
@@ -269,9 +301,11 @@
             mid_norm[at] = norm(total)
             partial[...] = total
 
-            @pl.loop(0, hidden // hidden_cols)
+            @pl.loop(0, n_head)
             def _(j):
-                hid = block(j, hidden_cols)
+                for turn, action in between[piece].items():
+                    pl.when(j == turn)(action)
+                hid = block(lax.rem(me // 2 * 2 + j, n_head), hidden_cols)
                 inner = gelu(matmul_nt(mid_norm[at], wup[l, hid])).astype(BF16)
                 partial[...] += matmul(inner, wdown[l, hid])
 
@@ -288,9 +322,10 @@
             for step in range(1, n_head):
                 out_copy(l, piece, step).wait()
 
-    for i in range(6):
+    greet(met.at[0], 0)
+    for i in range(ITEMS):
         send(0, i)
-        if i < 3:
+        if i <= QKV:
             to_sibling(0, i).start()
     send(1, QKV)
     send(1, OUT)
@@ -332,14 +367,15 @@
         pick[block(i, LANES)] = chosen_rows(LANES, i * LANES, slot)
 
     relay(0, 0)
+    for turn in range(rounds):
+        entered(turn)
     seq_send_rows(0, code_ref[...].astype(BF16))
     relay(0, 1)
     for group in range(n_head):
         v[group, :, LANES:] = jnp.ones((PATCH, LANES), BF16)
     mine_chip = me // 2
     other_chip = partner // 2
-    own(0, QKV).wait()
-    to_sibling(0, QKV).wait_recv()
+    near_ready(0, QKV)
     ready(0, 0)
     normalise(0, 0)
     keys_values(0, mine_chip, 0)
@@ -348,7 +384,8 @@
     keys_values(0, mine_chip, 1)
     queries(0, mine_chip)
     relay(0, QKV)
-    to_sibling(0, OUT).start()
+    for i in range(OUT, ITEMS):
+        to_sibling(0, i).start()
     seq_receive(0)
     codes[...] = got[...].astype(F32)
     turned = jnp.transpose(codes[...], (1, 0))
@@ -358,54 +395,68 @@
     def _(i):
         spread[block(i, LANES)] = chosen_rows(LANES, i * LANES, target)
 
-    def relay_out():
-        relay(0, OUT)
-        to_sibling(0, UP).start()
-        to_sibling(0, DOWN).start()
-
-    attend(mine_chip * 2, 2, {1: relay_out})
+    attend(mine_chip * 2, 2, {1: lambda: relay(0, OUT)})
     relay_other(0, QKV)
+    relay(0, UP[0])
     relay_other(0, OUT)
 
     @pl.loop(0, points // LANES)
     def _(i):
         keep[block(i, LANES)] = chosen_rows(LANES, i * LANES, kept)
 
-    relay(0, UP)
-    forward(0, QKV).wait_recv()
-    forward_other(0, QKV).wait_recv()
+    relay(0, DOWN[0])
+    far_ready(0, QKV)
     for i in range(2):
         keys_values(0, other_chip, i)
     queries(0, other_chip)
-
-    def relay_up_down():
-        relay_other(0, UP)
-        relay(0, DOWN)
-
-    attend(other_chip * 2, 2, {1: relay_up_down})
+    relay(0, UP[1])
+
+    def relay_last():
+        relay(0, DOWN[1])
+        relay_other(0, UP[0])
+
+    attend(other_chip * 2, 2, {1: relay_last})
+    relay_other(0, DOWN[0])
     to_sibling(1, QKV).start()
     to_sibling(1, OUT).start()
-    relay_other(0, DOWN)
-    relay(1, QKV)
     ready(0, OUT)
-    ready(0, UP)
-    ready(0, DOWN)
-    feed_forward(0)
-    send(1, UP)
-    to_sibling(1, UP).start()
+    for i in UP + DOWN:
+        near_ready(0, i)
+
+    def first_far():
+        far_ready(0, UP[0])
+        far_ready(0, DOWN[0])
+        relay_other(0, UP[1])
+
+    def last_far():
+        relay_other(0, DOWN[1])
+        far_ready(0, UP[1])
+        far_ready(0, DOWN[1])
+
+    feed_forward(
+        0,
+        (
+            {n_head // 2: first_far, n_head - 1: last_far},
+            {0: lambda: relay(1, QKV), 2: lambda: relay(1, OUT)},
+        ),
+    )
+    for i in range(OUT + 1, ITEMS):
+        send(1, i)
+        to_sibling(1, i).start()
+    out_wait(0)
+
+    seq_send_rows(1, cols[0])
     relay_other(1, QKV)
-    relay(1, OUT)
-    out_wait(0)
-
-    seq_send_rows(1, cols[0])
     relay_other(1, OUT)
     moved[...] = matmul(keep[...], cols[0]).astype(BF16)
     seq_receive(1)
     moved[...] = (moved[...].astype(F32) + matmul(spread[...], got[...])).astype(BF16)
 
-    for i in (0, 1, DOWN):
+    for i in range(2):
         send(1, i)
         to_sibling(1, i).start()
+    relay(1, UP[0])
+    relay(1, UP[1])
 
     @pl.loop(0, slots // LANES)
     def _(i):
@@ -414,7 +465,8 @@
         place_col = (both[:, 0:1] * BASE + both[:, 1:2]).astype(jnp.int32) - BASE
         pick[at] = chosen_cols(place_col, points)
 
-    relay(1, UP)
+    relay(1, DOWN[0])
+    relay(1, DOWN[1])
     relay(1, 0)
     relay(1, 1)
     ready(1, 0)
@@ -428,19 +480,18 @@
         keys_values(1, chip, 1)
     for chip in range(n_head // 2):
         queries(1, chip)
-    attend(
-        0,
-        n_head,
-        {
-            1: lambda: relay_other(1, UP),
-            2: lambda: relay(1, DOWN),
-            n_head - 1: lambda: relay_other(1, DOWN),
-        },
-    )
-    ready(1, OUT)
-    ready(1, UP)
-    ready(1, DOWN)
-    feed_forward(1)
+    def relay_ups():
+        for i in UP:
+            relay_other(1, i)
+
+    def relay_downs():
+        for i in DOWN:
+            relay_other(1, i)
+
+    attend(0, n_head, {1: relay_ups, 2: relay_downs})
+    for i in range(OUT, ITEMS):
+        ready(1, i)
+    feed_forward(1, ({}, {}))
 
     @pl.loop(0, points // LANES)
     def _(i):
@@ -463,7 +514,7 @@
     final_ref[...] = (moved[...].astype(F32) + matmul(spread[...], got[...])).astype(BF16)
 
     for l in range(2):
-        for i in range(6):
+        for i in range(ITEMS):
             if l == 0 or i >= QKV:
                 to_partner(l, i).wait_send()
                 to_sibling(l, i).wait_send()
@@ -520,9 +571,10 @@
             pltpu.VMEM((slots, cols), F32),
             pltpu.VMEM((256, width), F32),
             pltpu.VMEM((points, LANES), F32),
-            pltpu.SemaphoreType.DMA((layers, 6)),
-            pltpu.SemaphoreType.DMA((layers, 6, 5)),
-            pltpu.SemaphoreType.DMA((layers, 6, 5)),
+            pltpu.SemaphoreType.REGULAR((peers.bit_length() - 1,)),
+            pltpu.SemaphoreType.DMA((layers, ITEMS)),
+            pltpu.SemaphoreType.DMA((layers, ITEMS, 5)),
+            pltpu.SemaphoreType.DMA((layers, ITEMS, 5)),
             pltpu.SemaphoreType.DMA((layers, own_rows // 256, n_head)),
             pltpu.SemaphoreType.DMA((layers, own_rows // 256, n_head)),
             pltpu.SemaphoreType.DMA((3, peers)),

time: 114 us -> 106 us (0.930)
  Pallas kernels: 112 us -> 103 us
    pallas_call x1, Pallas kernels: 112 us -> 103 us  [on_device(): pl.pallas_call(functools.partial(program_kernel, n_head, peers, near, cap...]
where the time goes in v3:
time: 106 us; the launch traced here: 105 us
  Pallas kernels  103 us (97%)
  local copies, waits for them, and re-layouts  1.87 us (2%)
    pallas_call x1, Pallas kernels, on_device(): pl.pallas_call(functools.partial(program_kernel, n_head, peers, near, cap...  103 us

profile of v3, /device:TPU:0, one launch (start us, length us, event | category | flops | bytes accessed | tf_op | source)
XLA Modules:
  0.0 105.3 jit_solution(14915498601901875459)
XLA Ops:
  0.0 103.5 %point_layers.1 = bf16[2048,128]{1,0:T(8,128)(2,1)} custom-call(bf16[2048,128]{1,0:T(8,128)(2,1)} %x_ref.1, bf16[2,3,512,128]{3,2,1,0:T(8,128)(2,1)} %bitcast.2, bf16[2,128,512]{2,1,0:T(8,128)(2,1)} %wout_ref.1, bf16[2,512,512]{2,1,0:T(8,128)(2,1)} %wup_ref.1, bf16[2,512,512]{2,1,0:T(8,128)(2,1)} %wdown_ref.1, s32[1,2048]{1,0:T(1,128)} %bitcast.3), custom_call_target="tpu_custom_call" | custom-call | tf_op jit(solution)/shard_map/point_layers/pallas_call | solution.py:543
  103.5 1.9 %copy.8 = bf16[2048,128]{1,0:T(8,128)(2,1)} copy(bf16[2048,128]{1,0:T(8,128)(2,1)} %point_layers.1) | data formatting | bytes 1048576

commit v4 on v3

--- a/solution.py
+++ b/solution.py
@@ -301,13 +301,16 @@
             mid_norm[at] = norm(total)
             partial[...] = total
 
-            @pl.loop(0, n_head)
+            @pl.loop(0, n_head // 2)
             def _(j):
                 for turn, action in between[piece].items():
-                    pl.when(j == turn)(action)
-                hid = block(lax.rem(me // 2 * 2 + j, n_head), hidden_cols)
-                inner = gelu(matmul_nt(mid_norm[at], wup[l, hid])).astype(BF16)
-                partial[...] += matmul(inner, wdown[l, hid])
+                    pl.when(j == turn // 2)(action)
+                first = block(lax.rem(me // 2 * 2 + 2 * j, n_head), hidden_cols)
+                second = block(lax.rem(me // 2 * 2 + 2 * j + 1, n_head), hidden_cols)
+                raised = matmul_nt(mid_norm[at], wup[l, first])
+                later = matmul_nt(mid_norm[at], wup[l, second])
+                lowered = matmul(gelu(raised).astype(BF16), wdown[l, first])
+                partial[...] += lowered + matmul(gelu(later).astype(BF16), wdown[l, second])
 
             result[at] = partial[...].astype(BF16)
             for step in range(2, n_head):
@@ -366,11 +369,15 @@
     def _(i):
         pick[block(i, LANES)] = chosen_rows(LANES, i * LANES, slot)
 
-    relay(0, 0)
     for turn in range(rounds):
         entered(turn)
     seq_send_rows(0, code_ref[...].astype(BF16))
-    relay(0, 1)
+
+    @pl.loop(0, points // LANES)
+    def _(i):
+        keep[block(i, LANES)] = chosen_rows(LANES, i * LANES, kept)
+
+    relay(0, 0)
     for group in range(n_head):
         v[group, :, LANES:] = jnp.ones((PATCH, LANES), BF16)
     mine_chip = me // 2
@@ -379,13 +386,11 @@
     ready(0, 0)
     normalise(0, 0)
     keys_values(0, mine_chip, 0)
+    relay(0, 1)
     ready(0, 1)
     normalise(0, 1)
     keys_values(0, mine_chip, 1)
     queries(0, mine_chip)
-    relay(0, QKV)
-    for i in range(OUT, ITEMS):
-        to_sibling(0, i).start()
     seq_receive(0)
     codes[...] = got[...].astype(F32)
     turned = jnp.transpose(codes[...], (1, 0))
@@ -395,14 +400,13 @@
     def _(i):
         spread[block(i, LANES)] = chosen_rows(LANES, i * LANES, target)
 
+    relay(0, QKV)
+    for i in range(OUT, ITEMS):
+        to_sibling(0, i).start()
     attend(mine_chip * 2, 2, {1: lambda: relay(0, OUT)})
     relay_other(0, QKV)
     relay(0, UP[0])
     relay_other(0, OUT)
-
-    @pl.loop(0, points // LANES)
-    def _(i):
-        keep[block(i, LANES)] = chosen_rows(LANES, i * LANES, kept)
 
     relay(0, DOWN[0])
     far_ready(0, QKV)
@@ -450,10 +454,17 @@
     relay_other(1, OUT)
     moved[...] = matmul(keep[...], cols[0]).astype(BF16)
     seq_receive(1)
-    moved[...] = (moved[...].astype(F32) + matmul(spread[...], got[...])).astype(BF16)
+
+    def place_arrived(chip, i):
+        at = pl.ds(pl.multiple_of(chip * PATCH + i * chunk, chunk), chunk)
+        moved[at] = (moved[at].astype(F32) + matmul(spread[at], got[...])).astype(BF16)
 
     for i in range(2):
-        send(1, i)
+        place_arrived(other_chip, i)
+        to_partner(1, i).start()
+    for i in range(2):
+        place_arrived(mine_chip, i)
+        own(1, i).start()
         to_sibling(1, i).start()
     relay(1, UP[0])
     relay(1, UP[1])

time: 106 us -> 102 us (0.962)
  Pallas kernels: 103 us -> 100 us
    pallas_call x1, Pallas kernels: 103 us -> 100 us  [on_device(): pl.pallas_call(functools.partial(program_kernel, n_head, peers, near, cap...]
where the time goes in v4:
time: 102 us
  Pallas kernels  100 us (98%)
  local copies, waits for them, and re-layouts  1.87 us (2%)
    pallas_call x1, Pallas kernels, on_device(): pl.pallas_call(functools.partial(program_kernel, n_head, peers, near, cap...  100 us

profile of v4, /device:TPU:0, one launch (start us, length us, event | category | flops | bytes accessed | tf_op | source)
XLA Modules:
  0.0 101.9 jit_solution(10044335798194567524)
XLA Ops:
  0.0 100.0 %point_layers.1 = bf16[2048,128]{1,0:T(8,128)(2,1)} custom-call(bf16[2048,128]{1,0:T(8,128)(2,1)} %x_ref.1, bf16[2,3,512,128]{3,2,1,0:T(8,128)(2,1)} %bitcast.2, bf16[2,128,512]{2,1,0:T(8,128)(2,1)} %wout_ref.1, bf16[2,512,512]{2,1,0:T(8,128)(2,1)} %wup_ref.1, bf16[2,512,512]{2,1,0:T(8,128)(2,1)} %wdown_ref.1, s32[1,2048]{1,0:T(1,128)} %bitcast.3), custom_call_target="tpu_custom_call" | custom-call | tf_op jit(solution)/shard_map/point_layers/pallas_call | solution.py:554
  100.0 1.9 %copy.8 = bf16[2048,128]{1,0:T(8,128)(2,1)} copy(bf16[2048,128]{1,0:T(8,128)(2,1)} %point_layers.1) | data formatting | bytes 1048576

commit v5 on v4

--- a/solution.py
+++ b/solution.py
@@ -50,10 +50,11 @@
     return (slots == index_col).astype(F32).astype(BF16)
 
 
-QKV, OUT = 2, 3
-UP = (4, 6)
-DOWN = (5, 7)
-ITEMS = 8
+CHUNKS = 4
+QKV, OUT = CHUNKS, CHUNKS + 1
+UP = (CHUNKS + 2, CHUNKS + 4)
+DOWN = (CHUNKS + 3, CHUNKS + 5)
+ITEMS = CHUNKS + 6
 
 
 def program_kernel(
@@ -61,7 +62,7 @@
     x_ref, wqkv_ref, wout_ref, wup_ref, wdown_ref, index_ref,
     final_ref,
     rows, wqkv, wout, wup, wdown, normed, q, k, v, attended, mid_norm, result, cols, moved,
-    pick, keep, spread, near_out, far_out, near_in, far_in, got, codes, partial, code_ref,
+    pick, early, keep, spread, near_out, far_out, near_in, far_in, got, codes, partial, code_ref,
     met, local_sem, send_sem, recv_sem, out_send, out_recv, seq_send, seq_recv,
 ):
     me = lax.axis_index("head")
@@ -72,7 +73,7 @@
     own_rows, width = result.shape
     points = moved.shape[0]
     slots = 2 * near + peers * cap
-    chunk = PATCH // 2
+    chunk = PATCH // CHUNKS
 
     barrier = pltpu.get_barrier_semaphore()
     for step in range(1, n_head):
@@ -105,7 +106,7 @@
     hidden_half = hidden // n_head // 2
 
     def source(l, i, to):
-        if i < 2:
+        if i < CHUNKS:
             start = pl.multiple_of((to // 2) * PATCH + i * chunk, chunk)
             return (x_ref if l == 0 else moved).at[pl.ds(start, chunk)]
         if i in (QKV, OUT):
@@ -114,7 +115,7 @@
         return ref.at[l, pl.ds(turn * hidden_half, hidden_half)]
 
     def place(l, i, owner):
-        if i < 2:
+        if i < CHUNKS:
             return rows.at[l, pl.ds(i * chunk, chunk), block(owner, LANES)]
         if i == QKV:
             return wqkv.at[l, owner // 2, :, :, block(lax.rem(owner, 2), LANES)]
@@ -124,7 +125,7 @@
         return ref.at[l, block((owner // 2 * 2 + turn) * 2 + lax.rem(owner, 2), hidden_half)]
 
     def part(i, ref, which):
-        if i < 2:
+        if i < CHUNKS:
             return ref
         if i == QKV:
             return ref.at[:, block(which, ref.shape[1] // 2)]
@@ -209,15 +210,23 @@
             device_id_type=MESH,
         )
 
-    def seq_send_rows(turn, table):
+    def seq_send_rows(turn, found):
         for lo in range(0, 2 * near, near):
-            near_out[turn, lo : lo + near] = matmul(pick[lo : lo + near], table).astype(BF16)
+            near_out[turn, lo : lo + near] = found(lo, lo + near).astype(BF16)
             seq_copy(turn, (1 if lo == 0 else peers - 1) if turn != 2 else (peers - 1 if lo == 0 else 1)).start()
-        packed = matmul(pick[2 * near :], table)
+        packed = found(2 * near, slots)
         for peer in range(peers):
             far_out[turn, peer] = packed[peer * cap : (peer + 1) * cap].astype(BF16)
         for step in range(2, peers - 1):
             seq_copy(turn, step).start()
+
+    def picked(l, piece, lo, hi):
+        found = None
+        for start in range(piece * 256, points, own_rows):
+            at = slice(start, start + 256)
+            term = matmul(pick[lo:hi, at], cols[l, at])
+            found = term if found is None else found + term
+        return found
 
     def seq_receive(turn):
         for step in range(1, peers):
@@ -320,10 +329,18 @@
                 at, block(me, LANES)
             ]
 
+    pieces = own_rows // 256
+
     def out_wait(l):
-        for piece in range(own_rows // 256):
+        for piece in range(pieces):
             for step in range(1, n_head):
                 out_copy(l, piece, step).wait()
+            if piece + 1 < pieces:
+                found = picked(l, piece, 0, slots)
+                early[...] = found if piece == 0 else early[...] + found
+
+    def last_picked(l):
+        return lambda lo, hi: early[lo:hi] + picked(l, pieces - 1, lo, hi)
 
     greet(met.at[0], 0)
     for i in range(ITEMS):
@@ -371,7 +388,7 @@
 
     for turn in range(rounds):
         entered(turn)
-    seq_send_rows(0, code_ref[...].astype(BF16))
+    seq_send_rows(0, lambda lo, hi: matmul(pick[lo:hi], code_ref[...].astype(BF16)))
 
     @pl.loop(0, points // LANES)
     def _(i):
@@ -383,13 +400,12 @@
     mine_chip = me // 2
     other_chip = partner // 2
     near_ready(0, QKV)
-    ready(0, 0)
-    normalise(0, 0)
-    keys_values(0, mine_chip, 0)
-    relay(0, 1)
-    ready(0, 1)
-    normalise(0, 1)
-    keys_values(0, mine_chip, 1)
+    for i in range(CHUNKS):
+        if i + 1 < CHUNKS:
+            relay(0, i + 1)
+        ready(0, i)
+        normalise(0, i)
+        keys_values(0, mine_chip, i)
     queries(0, mine_chip)
     seq_receive(0)
     codes[...] = got[...].astype(F32)
@@ -410,7 +426,7 @@
 
     relay(0, DOWN[0])
     far_ready(0, QKV)
-    for i in range(2):
+    for i in range(CHUNKS):
         keys_values(0, other_chip, i)
     queries(0, other_chip)
     relay(0, UP[1])
@@ -449,7 +465,7 @@
         to_sibling(1, i).start()
     out_wait(0)
 
-    seq_send_rows(1, cols[0])
+    seq_send_rows(1, last_picked(0))
     relay_other(1, QKV)
     relay_other(1, OUT)
     moved[...] = matmul(keep[...], cols[0]).astype(BF16)
@@ -459,10 +475,10 @@
         at = pl.ds(pl.multiple_of(chip * PATCH + i * chunk, chunk), chunk)
         moved[at] = (moved[at].astype(F32) + matmul(spread[at], got[...])).astype(BF16)
 
-    for i in range(2):
+    for i in range(CHUNKS):
         place_arrived(other_chip, i)
         to_partner(1, i).start()
-    for i in range(2):
+    for i in range(CHUNKS):
         place_arrived(mine_chip, i)
         own(1, i).start()
         to_sibling(1, i).start()
@@ -479,16 +495,15 @@
     relay(1, DOWN[0])
     relay(1, DOWN[1])
     relay(1, 0)
-    relay(1, 1)
-    ready(1, 0)
-    normalise(1, 0)
-    ready(1, QKV)
-    for chip in range(n_head // 2):
-        keys_values(1, chip, 0)
-    ready(1, 1)
-    normalise(1, 1)
-    for chip in range(n_head // 2):
-        keys_values(1, chip, 1)
+    for i in range(CHUNKS):
+        if i + 1 < CHUNKS:
+            relay(1, i + 1)
+        ready(1, i)
+        normalise(1, i)
+        if i == 0:
+            ready(1, QKV)
+        for chip in range(n_head // 2):
+            keys_values(1, chip, i)
     for chip in range(n_head // 2):
         queries(1, chip)
     def relay_ups():
@@ -510,7 +525,7 @@
         keep[at] = chosen_cols(code_ref[at, 3:4].astype(jnp.int32), points)
 
     out_wait(1)
-    seq_send_rows(2, cols[1])
+    seq_send_rows(2, last_picked(1))
 
     @pl.loop(0, points // LANES)
     def _(i):
@@ -572,6 +587,7 @@
             pltpu.VMEM((layers, points, cols), BF16),
             pltpu.VMEM((points, cols), BF16),
             pltpu.VMEM((slots, points), BF16),
+            pltpu.VMEM((slots, cols), F32),
             pltpu.VMEM((points, points), BF16),
             pltpu.VMEM((points, slots), BF16),
             pltpu.VMEM((3, 2 * near, cols), BF16),

time: 102 us -> 100 us (0.980)
  Pallas kernels: 100 us -> 98.3 us
    pallas_call x1, Pallas kernels: 100 us -> 98.3 us  [on_device(): pl.pallas_call(functools.partial(program_kernel, n_head, peers, near, cap...]
where the time goes in v5:
time: 100 us
  Pallas kernels  98.3 us (98%)
  local copies, waits for them, and re-layouts  1.87 us (2%)
    pallas_call x1, Pallas kernels, on_device(): pl.pallas_call(functools.partial(program_kernel, n_head, peers, near, cap...  98.3 us

profile of v5, /device:TPU:0, one launch (start us, length us, event | category | flops | bytes accessed | tf_op | source)
XLA Modules:
  0.0 100.2 jit_solution(15749819685368014993)
XLA Ops:
  0.0 98.3 %point_layers.1 = bf16[2048,128]{1,0:T(8,128)(2,1)} custom-call(bf16[2048,128]{1,0:T(8,128)(2,1)} %x_ref.1, bf16[2,3,512,128]{3,2,1,0:T(8,128)(2,1)} %bitcast.2, bf16[2,128,512]{2,1,0:T(8,128)(2,1)} %wout_ref.1, bf16[2,512,512]{2,1,0:T(8,128)(2,1)} %wup_ref.1, bf16[2,512,512]{2,1,0:T(8,128)(2,1)} %wdown_ref.1, s32[1,2048]{1,0:T(1,128)} %bitcast.3), custom_call_target="tpu_custom_call" | custom-call | tf_op jit(solution)/shard_map/point_layers/pallas_call | solution.py:569
  98.3 1.9 %copy.8 = bf16[2048,128]{1,0:T(8,128)(2,1)} copy(bf16[2048,128]{1,0:T(8,128)(2,1)} %point_layers.1) | data formatting | bytes 1048576
